TPU v7x, 32 devices: a whole 2x2x4 slice. The times are simulated.
32 devices in a mesh: ctx: 4 (over y, core), head: 2 (over x), batch: 4 (over z).
Axes of the slice: x: 2, y: 2, z: 4, core: 2. Of those that a mesh axis runs over, the one named last changes fastest.
Arguments:
- ingest: bfloat16 [4, 4, 12, 128, 4, 256], P('ctx', 'batch', None, None, None, 'head'), may hold values from -6 to 6
- src_shard: int32 [4, 4, 6], P('ctx'), may hold values from 0 to 3, as said below
- src_slot: int32 [4, 4, 6], P('ctx'), may hold values from 0 to 11
- hist_len: int32 [4, 4], P('batch'), may hold values from 1 to 1536, 3072 in all within a row
- w_out: bfloat16 [256, 256], P('head'), may hold values from -0.375 to 0.375
Outputs:
- mixed: bfloat16 [4, 3072, 256], P('batch', 'ctx', 'head')
Inputs may be any that keep to these rules, and one draw needn't show every extreme that they name: `src_shard`: for each owner index, every owner's 6 blocks come from exactly two different ingestion shards, 3 from each; no (shard, slot) pair of one owner index feeds two blocks. `hist_len`: the 4 histories of a group fill its 3072 positions in order.
All inputs are finite; a program needn't handle non-finite values.
Results may differ from a plain program's by a relative error of at most 0.0058.
Values may be sent and summed in bfloat16 or wider, within the bound.
A program may use at most 64 MiB of HBM per device.

v0:
```python
import math

import jax
import jax.numpy as jnp
from jax import lax
from jax.sharding import PartitionSpec as P

HD = 128


key_block = 512


def body(ingest, src_shard, src_slot, hist_len, w_out):
    groups = lax.axis_size("batch")
    me_batch = lax.axis_index("batch")
    ingested = ingest[0, 0]
    slot_total, block_rows, kinds, local_width = ingested.shape
    shards = src_shard[0]
    slot_ids = src_slot[0]
    per_owner = shards.shape[1]
    capacity = per_owner // 2
    matching = shards == me_batch
    sender_rank = jnp.cumsum(matching.astype(jnp.int32), axis=1) - 1
    slot_order = jnp.arange(capacity, dtype=jnp.int32)
    picked = matching[:, :, None] & (sender_rank[:, :, None] == slot_order[None, None, :])
    send_slot = jnp.sum(jnp.where(picked, slot_ids[:, :, None], 0), axis=1)
    send_live = jnp.any(picked, axis=1)
    outgoing = jnp.take(ingested, send_slot.reshape(-1), axis=0)
    outgoing = outgoing.reshape(groups, capacity, block_rows, kinds, local_width)
    outgoing = jnp.where(send_live[:, :, None, None, None], outgoing, jnp.zeros_like(outgoing))
    incoming = lax.all_to_all(outgoing, "batch", split_axis=0, concat_axis=0, tiled=True)
    owner_flags = jnp.arange(groups, dtype=jnp.int32) == me_batch
    own_sources = jnp.sum(jnp.where(owner_flags[:, None], shards, 0), axis=0)
    block_pos = jnp.arange(per_owner)
    earlier = (own_sources[None, :] == own_sources[:, None]) & (
        block_pos[None, :] < block_pos[:, None]
    )
    arrival = jnp.sum(earlier.astype(jnp.int32), axis=1)
    flat_index = own_sources * capacity + arrival
    owned = jnp.take(
        incoming.reshape(groups * capacity, block_rows, kinds, local_width), flat_index, axis=0
    )
    row_count = per_owner * block_rows
    owned = owned.reshape(row_count, kinds, local_width)
    heads_local = local_width // HD
    queries = owned[:, 0].reshape(row_count, heads_local, HD)
    key_part = owned[:, 1]
    value_part = owned[:, 2]
    update_rows = owned[:, 3].reshape(row_count, heads_local, HD)
    query_pos = lax.axis_index("ctx") * row_count + jnp.arange(row_count, dtype=jnp.int32)
    seg_ends = jnp.cumsum(hist_len[0])

    def segment_of(positions):
        return jnp.sum((positions[:, None] >= seg_ends[None, :]).astype(jnp.int32), axis=1)

    query_seg = segment_of(query_pos)
    score_scale = 1.0 / math.sqrt(HD)

    def tile_update(running, key_rows, value_rows, offset):
        key_count = key_rows.shape[0]
        key_pos = offset + jnp.arange(key_count, dtype=jnp.int32)
        visible = (query_seg[:, None] == segment_of(key_pos)[None, :]) & (
            key_pos[None, :] <= query_pos[:, None]
        )
        key_heads = key_rows.reshape(key_count, heads_local, HD)
        value_heads = value_rows.reshape(key_count, heads_local, HD)
        scores = (
            jnp.einsum("qhd,khd->hqk", queries, key_heads, preferred_element_type=jnp.float32)
            * score_scale
        )
        weights = jnp.where(visible[None], jax.nn.silu(scores), 0.0).astype(jnp.bfloat16)
        return running + jnp.einsum(
            "hqk,khd->qhd", weights, value_heads, preferred_element_type=jnp.float32
        )

    empty = jnp.zeros((row_count, heads_local, HD), jnp.float32)
    key_rows = lax.all_gather(key_part, "ctx", axis=0, tiled=True)
    value_rows = lax.all_gather(value_part, "ctx", axis=0, tiled=True)
    key_count = key_rows.shape[0]
    blocks = key_count // key_block
    key_blocks = key_rows.reshape(blocks, key_block, key_rows.shape[1])
    value_blocks = value_rows.reshape(blocks, key_block, value_rows.shape[1])
    block_offsets = key_block * jnp.arange(blocks, dtype=jnp.int32)

    def step_block(carry, block_args):
        key_tile, value_tile, tile_offset = block_args
        return (tile_update(carry, key_tile, value_tile, tile_offset), None)

    attended = lax.scan(step_block, empty, (key_blocks, value_blocks, block_offsets))[0]
    mean_square = jnp.mean(attended * attended, axis=-1, keepdims=True)
    normed = attended * lax.rsqrt(mean_square + 1e-06)
    gated_out = (
        (normed * update_rows.astype(jnp.float32))
        .astype(jnp.bfloat16)
        .reshape(row_count, local_width)
    )
    column_block = lax.all_to_all(w_out, "head", split_axis=1, concat_axis=0, tiled=True)
    mixed_rows = jnp.dot(
        lax.all_gather(gated_out, "head", axis=1, tiled=True),
        column_block,
        preferred_element_type=jnp.float32,
    )
    return mixed_rows.astype(jnp.bfloat16)[None]


def solution(mesh):
    in_specs = (
        P("ctx", "batch", None, None, None, "head"),
        P("ctx", None, None),
        P("ctx", None, None),
        P("batch", None),
        P("head", None),
    )
    out_specs = P("batch", "ctx", "head")
    return jax.shard_map(body, mesh=mesh, in_specs=in_specs, out_specs=out_specs, check_vma=False)
```

profile of v0, /device:TPU:0, one launch (start us, length us, event | category | flops | bytes accessed | tf_op | source)
XLA Modules:
  0.0 109.1 jit_solution(9288471767603414013)
XLA Ops:
  0.0 1.7 %copy.23 = bf16[128,256]{0,1:T(8,128)(2,1)} copy(bf16[128,256]{1,0:T(8,128)(2,1)} %param.11) | data formatting | bytes 131072 | tf_op args[4]
  1.7 4.2 %all-to-all-start.1 = ((bf16[128,2,128]{0,2,1:T(8,128)(2,1)}), bf16[128,2,128]{0,2,1:T(8,128)(2,1)S(1)}, u32[]{:S(2)}, u32[]{:S(2)}) async-start(bf16[128,2,128]{0,2,1:T(8,128)(2,1)} %bitcast.15), calls=%async_computation.1 | async-start | bytes 131072 | tf_op jit(solution)/shard_map/all_to_all | solution.py:98
  5.9 0.7 fusion.39
  6.6 0.2 reduce_window_sum.18
  6.8 0.8 select_reduce_fusion
  7.6 0.1 copy.19
  7.7 0.2 fusion.35
  8.0 0.1 copy.18
  8.1 0.1 copy.17
  8.2 1.9 %gather_fusion = bf16[12,128,4,128]{3,2,1,0:T(4,128)(2,1)S(1)} fusion(bf16[12,128,4,128]{3,2,1,0:T(4,128)(2,1)S(1)} %bitcast.84, s32[1024]{0:T(1024)S(1)} %pad_clamp_fusion.1), kind=kCustom, calls=%fused_computation | custom fusion | bytes 3145776 | tf_op jit(solution)/shard_map/jit(_take)/gather | solution.py:29
  10.1 1.4 %fusion.30 = bf16[4,3,128,4,128]{4,2,3,1,0:T(8,128)(2,1)} fusion(bf16[4,3,128,4,128]{4,3,2,1,0:T(4,128)(2,1)S(1)} %bitcast.85, pred[4,3]{1,0:T(4,128)(4,1)S(1)} %copy.18, pred[4,3]{1,0:T(4,128)(4,1)S(1)} %copy.17), kind=kLoop, calls=%fused_computation.33 | loop fusion | flops 1572864 | bytes 3145752 | tf_op jit(solution)/shard_map/jit(_where)/select_n | solution.py:31
  11.6 0.6 copy-done.2
  12.2 5.4 %all-to-all-start = ((bf16[4,3,128,4,128]{4,2,3,1,0:T(8,128)(2,1)}), bf16[4,3,128,4,128]{4,2,3,1,0:T(8,128)(2,1)S(1)}, u32[]{:S(2)}, u32[]{:S(2)}) async-start(bf16[4,3,128,4,128]{4,2,3,1,0:T(8,128)(2,1)} %fusion.30), calls=%async_computation | async-start | bytes 3145728 | tf_op jit(solution)/shard_map/all_to_all | solution.py:32
  17.6 0.2 reduce-window.8
  17.8 0.5 iota_multiply_fusion
  18.4 0.2 convert_reduce_fusion.2
  18.7 0.7 convert_reduce_fusion.1
  19.4 1.6 %copy.24 = bf16[2,128,128]{2,1,0:T(8,128)(2,1)} copy(bf16[2,128,128]{1,2,0:T(8,128)(2,1)} %bitcast.90) | data formatting | bytes 131072 | tf_op jit(solution)/shard_map/all_to_all | solution.py:98
  21.0 33.6 %all-to-all-done = bf16[4,3,128,4,128]{4,2,3,1,0:T(8,128)(2,1)S(1)} async-done(((bf16[4,3,128,4,128]{4,2,3,1,0:T(8,128)(2,1)}), bf16[4,3,128,4,128]{4,2,3,1,0:T(8,128)(2,1)S(1)}, u32[]{:S(2)}, u32[]{:S(2)}) %all-to-all-start) | async-done | bytes 1572896 | tf_op jit(solution)/shard_map/all_to_all | solution.py:32
  54.6 1.5 %gather_fusion.1 = bf16[6,128,4,128]{3,1,2,0:T(8,128)(2,1)} fusion(bf16[12,128,4,128]{3,1,2,0:T(8,128)(2,1)S(1)} %bitcast.86, s32[1024]{0:T(1024)S(1)} %pad_clamp_fusion), kind=kCustom, calls=%fused_computation.1 | custom fusion | bytes 1572888 | tf_op jit(solution)/shard_map/jit(_take)/gather | solution.py:41
  56.1 1.2 %copy.21 = bf16[6,128,4,128]{3,1,0,2:T(8,128)(2,1)S(1)} copy(bf16[6,128,4,128]{3,1,2,0:T(8,128)(2,1)} %gather_fusion.1) | data formatting | bytes 1572864 | tf_op jit(solution)/shard_map/jit(_take)/gather | solution.py:41
  57.3 0.2 bitcast_select_fusion
  57.5 0.7 fusion.40
  58.2 8.6 %all-gather = bf16[3072,1,128]{2,0,1:T(8,128)(2,1)S(1)} all-gather(bf16[768,1,128]{2,0,1:T(8,128)(2,1)S(1)} %get-tuple-element.117), channel_id=2, replica_groups=mesh['ctx'=4,'head'=2,'batch'=4] {'ctx'}, dimensions={0}, use_global_device_ids=true | all-gather | bytes 983040 | tf_op jit(solution)/shard_map/all_gather | solution.py:79
  66.8 9.1 %all-gather.1 = bf16[3072,1,128]{2,0,1:T(8,128)(2,1)} all-gather(bf16[768,1,128]{2,0,1:T(8,128)(2,1)S(1)} %get-tuple-element.116), channel_id=3, replica_groups=mesh['ctx'=4,'head'=2,'batch'=4] {'ctx'}, dimensions={0}, use_global_device_ids=true | all-gather | bytes 983040 | tf_op jit(solution)/shard_map/all_gather | solution.py:78
  76.0 23.9 %while.11 = (s32[]{:T(128)}, f32[768,1,128]{0,2,1:T(8,128)S(1)}, bf16[6,512,128]{2,1,0:T(8,128)(2,1)S(1)}, s32[768]{0:T(1024)}, s32[6]{0:T(128)}, /*index=5*/s32...) while((s32[]{:T(128)}, f32[768,1,128]{0,2,1:T(8,128)S(1)}, ...), condition=%wide.region_9.10_spmd.clone, body=%wide.region_7.9_spmd.clone.sunk | while | flops 205462272 | bytes 1267867 | solution.py:90
  76.0 1.3 %dynamic_slice.28 = s32[1]{0:T(128)} dynamic-slice(s32[6]{0:T(128)} %get-tuple-element.199, s32[]{:T(128)} %get-tuple-element.184), dynamic_slice_sizes={1} | dynamic-slice | bytes 12 | tf_op jit(solution)/shard_map/while/body/jit(dynamic_index_in_dim)/dynamic_slice | solution.py:90
  77.2 0.6 iota_add_fusion.6
  78.0 2.0 %fusion.49 = f32[768,1,128]{0,2,1:T(8,128)S(1)} fusion(s32[768]{0:T(1024)S(1)} %iota_add_fusion.5, s32[768]{0:T(1024)} %get-tuple-element.198, s32[512]{0:T(512)S(1)} %iota_add_fusion.6, s32[512]{0:T(512)S(1)} %convert_reduce_fusion.4, f32[768,1,128]{0,2,1:T(8,128)S(1)} %get-tuple-element.185, bf16[768,1,128]{2,0,1:T(8,128)(2,1)} %get-tuple-element.202, ...), kind=kOutput, calls=%fused_computation.12.clone.1 | convolution fusion | flops 205455360 | bytes 1258497 | tf_op jit(solution)/shard_map/while/body/eval_jaxpr/hqk,khd->qhd/dot_general | solution.py:73
  80.0 1.3 %dynamic_slice.28 = s32[1]{0:T(128)} dynamic-slice(s32[6]{0:T(128)} %get-tuple-element.199, s32[]{:T(128)} %get-tuple-element.184), dynamic_slice_sizes={1} | dynamic-slice | bytes 12 | tf_op jit(solution)/shard_map/while/body/jit(dynamic_index_in_dim)/dynamic_slice | solution.py:90
  81.2 0.6 iota_add_fusion.6
  82.0 2.0 %fusion.49 = f32[768,1,128]{0,2,1:T(8,128)S(1)} fusion(s32[768]{0:T(1024)S(1)} %iota_add_fusion.5, s32[768]{0:T(1024)} %get-tuple-element.198, s32[512]{0:T(512)S(1)} %iota_add_fusion.6, s32[512]{0:T(512)S(1)} %convert_reduce_fusion.4, f32[768,1,128]{0,2,1:T(8,128)S(1)} %get-tuple-element.185, bf16[768,1,128]{2,0,1:T(8,128)(2,1)} %get-tuple-element.202, ...), kind=kOutput, calls=%fused_computation.12.clone.1 | convolution fusion | flops 205455360 | bytes 1258497 | tf_op jit(solution)/shard_map/while/body/eval_jaxpr/hqk,khd->qhd/dot_general | solution.py:73
  83.9 1.3 %dynamic_slice.28 = s32[1]{0:T(128)} dynamic-slice(s32[6]{0:T(128)} %get-tuple-element.199, s32[]{:T(128)} %get-tuple-element.184), dynamic_slice_sizes={1} | dynamic-slice | bytes 12 | tf_op jit(solution)/shard_map/while/body/jit(dynamic_index_in_dim)/dynamic_slice | solution.py:90
  85.2 0.6 iota_add_fusion.6
  85.9 2.0 %fusion.49 = f32[768,1,128]{0,2,1:T(8,128)S(1)} fusion(s32[768]{0:T(1024)S(1)} %iota_add_fusion.5, s32[768]{0:T(1024)} %get-tuple-element.198, s32[512]{0:T(512)S(1)} %iota_add_fusion.6, s32[512]{0:T(512)S(1)} %convert_reduce_fusion.4, f32[768,1,128]{0,2,1:T(8,128)S(1)} %get-tuple-element.185, bf16[768,1,128]{2,0,1:T(8,128)(2,1)} %get-tuple-element.202, ...), kind=kOutput, calls=%fused_computation.12.clone.1 | convolution fusion | flops 205455360 | bytes 1258497 | tf_op jit(solution)/shard_map/while/body/eval_jaxpr/hqk,khd->qhd/dot_general | solution.py:73
  87.9 1.3 %dynamic_slice.28 = s32[1]{0:T(128)} dynamic-slice(s32[6]{0:T(128)} %get-tuple-element.199, s32[]{:T(128)} %get-tuple-element.184), dynamic_slice_sizes={1} | dynamic-slice | bytes 12 | tf_op jit(solution)/shard_map/while/body/jit(dynamic_index_in_dim)/dynamic_slice | solution.py:90
  89.2 0.6 iota_add_fusion.6
  89.9 2.0 %fusion.49 = f32[768,1,128]{0,2,1:T(8,128)S(1)} fusion(s32[768]{0:T(1024)S(1)} %iota_add_fusion.5, s32[768]{0:T(1024)} %get-tuple-element.198, s32[512]{0:T(512)S(1)} %iota_add_fusion.6, s32[512]{0:T(512)S(1)} %convert_reduce_fusion.4, f32[768,1,128]{0,2,1:T(8,128)S(1)} %get-tuple-element.185, bf16[768,1,128]{2,0,1:T(8,128)(2,1)} %get-tuple-element.202, ...), kind=kOutput, calls=%fused_computation.12.clone.1 | convolution fusion | flops 205455360 | bytes 1258497 | tf_op jit(solution)/shard_map/while/body/eval_jaxpr/hqk,khd->qhd/dot_general | solution.py:73
  91.9 1.3 %dynamic_slice.28 = s32[1]{0:T(128)} dynamic-slice(s32[6]{0:T(128)} %get-tuple-element.199, s32[]{:T(128)} %get-tuple-element.184), dynamic_slice_sizes={1} | dynamic-slice | bytes 12 | tf_op jit(solution)/shard_map/while/body/jit(dynamic_index_in_dim)/dynamic_slice | solution.py:90
  93.2 0.6 iota_add_fusion.6
  93.9 2.0 %fusion.49 = f32[768,1,128]{0,2,1:T(8,128)S(1)} fusion(s32[768]{0:T(1024)S(1)} %iota_add_fusion.5, s32[768]{0:T(1024)} %get-tuple-element.198, s32[512]{0:T(512)S(1)} %iota_add_fusion.6, s32[512]{0:T(512)S(1)} %convert_reduce_fusion.4, f32[768,1,128]{0,2,1:T(8,128)S(1)} %get-tuple-element.185, bf16[768,1,128]{2,0,1:T(8,128)(2,1)} %get-tuple-element.202, ...), kind=kOutput, calls=%fused_computation.12.clone.1 | convolution fusion | flops 205455360 | bytes 1258497 | tf_op jit(solution)/shard_map/while/body/eval_jaxpr/hqk,khd->qhd/dot_general | solution.py:73
  95.9 1.3 %dynamic_slice.28 = s32[1]{0:T(128)} dynamic-slice(s32[6]{0:T(128)} %get-tuple-element.199, s32[]{:T(128)} %get-tuple-element.184), dynamic_slice_sizes={1} | dynamic-slice | bytes 12 | tf_op jit(solution)/shard_map/while/body/jit(dynamic_index_in_dim)/dynamic_slice | solution.py:90
  97.2 0.6 iota_add_fusion.6
  97.9 2.0 %fusion.49 = f32[768,1,128]{0,2,1:T(8,128)S(1)} fusion(s32[768]{0:T(1024)S(1)} %iota_add_fusion.5, s32[768]{0:T(1024)} %get-tuple-element.198, s32[512]{0:T(512)S(1)} %iota_add_fusion.6, s32[512]{0:T(512)S(1)} %convert_reduce_fusion.4, f32[768,1,128]{0,2,1:T(8,128)S(1)} %get-tuple-element.185, bf16[768,1,128]{2,0,1:T(8,128)(2,1)} %get-tuple-element.202, ...), kind=kOutput, calls=%fused_computation.12.clone.1 | convolution fusion | flops 205455360 | bytes 1258497 | tf_op jit(solution)/shard_map/while/body/eval_jaxpr/hqk,khd->qhd/dot_general | solution.py:73
  99.9 0.2 copy.22
  100.1 0.2 multiply_convert_fusion
  100.3 7.8 %all-gather.2 = bf16[768,1,256]{2,0,1:T(8,128)(2,1)S(1)} all-gather(bf16[768,1,128]{2,0,1:T(8,128)(2,1)S(1)} %multiply_convert_fusion), channel_id=4, replica_groups=mesh['ctx'=4,'head'=2,'batch'=4] {'head'}, dimensions={2}, use_global_device_ids=true | all-gather | bytes 589824 | tf_op jit(solution)/shard_map/all_gather | solution.py:100
  108.1 0.9 fusion.31
  (37 shorter events, 0.9 us)
Async XLA Ops:
  0.0 8.2 %copy-start = (bf16[1,1,12,128,4,128]{5,4,3,2,1,0:T(4,128)(2,1)S(1)}, bf16[1,1,12,128,4,128]{5,4,3,2,1,0:T(4,128)(2,1)}, u32[]{:S(2)}) copy-start(bf16[1,1,12,128,4,128]{5,4,3,2,1,0:T(4,128)(2,1)} %param.7) | copy-start | bytes 4718596
  1.7 9.9 %all-to-all-start.1 = ((bf16[128,2,128]{0,2,1:T(8,128)(2,1)}), bf16[128,2,128]{0,2,1:T(8,128)(2,1)S(1)}, u32[]{:S(2)}, u32[]{:S(2)}) async-start(bf16[128,2,128]{0,2,1:T(8,128)(2,1)} %bitcast.15), calls=%async_computation.1 | async-start | bytes 131072 | tf_op jit(solution)/shard_map/all_to_all | solution.py:98
  11.6 6.1 %copy-start.4 = (s32[1,4]{1,0:T(1,128)S(1)}, s32[1,4]{1,0:T(1,128)}, u32[]{:S(2)}) copy-start(s32[1,4]{1,0:T(1,128)} %param.10) | copy-start | bytes 52
  11.6 6.8 %copy-start.3 = (s32[1,4,6]{2,1,0:T(4,128)S(1)}, s32[1,4,6]{2,1,0:T(4,128)}, u32[]{:S(2)}) copy-start(s32[1,4,6]{2,1,0:T(4,128)} %param.8) | copy-start | bytes 292
  11.6 0.6 copy-start.2
  12.2 42.4 %all-to-all-start = ((bf16[4,3,128,4,128]{4,2,3,1,0:T(8,128)(2,1)}), bf16[4,3,128,4,128]{4,2,3,1,0:T(8,128)(2,1)S(1)}, u32[]{:S(2)}, u32[]{:S(2)}) async-start(bf16[4,3,128,4,128]{4,2,3,1,0:T(8,128)(2,1)} %fusion.30), calls=%async_computation | async-start | bytes 3145728 | tf_op jit(solution)/shard_map/all_to_all | solution.py:32
  99.9 8.3 %copy-start.1 = (bf16[2,128,128]{2,1,0:T(8,128)(2,1)S(1)}, bf16[2,128,128]{2,1,0:T(8,128)(2,1)}, u32[]{:S(2)}) copy-start(bf16[2,128,128]{2,1,0:T(8,128)(2,1)} %copy.24) | copy-start | bytes 196612
where the time goes:
time: 110 us; the launch traced here: 109 us
  waiting for transfers between devices  33.6 us (31%)
  blocking collectives  25.6 us (23%)
  local copies, waits for them, and re-layouts  17.5 us (16%)
  matrix products  12.7 us (12%)
  other arithmetic  9.72 us (9%)
  starting transfers between devices  9.66 us (9%)
    all_to_all x1, waiting for transfers between devices, body(): lax.all_to_all(outgoing, 'batch', split_axis=0, concat_axis=0, tiled=True)  33.6 us
    dot_general x6, matrix products, tile_update(): jnp.einsum('hqk,khd->qhd', weights, value_heads, preferred_element_type=j...  11.8 us
    all_gather x1, blocking collectives, body(): key_rows = lax.all_gather(key_part, 'ctx', axis=0, tiled=True)  9.14 us
    all_gather x1, blocking collectives, body(): value_rows = lax.all_gather(value_part, 'ctx', axis=0, tiled=True)  8.61 us
    all_gather x1, blocking collectives, body(): lax.all_gather(gated_out, 'head', axis=1, tiled=True)  7.84 us
    dynamic_slice x6, local copies, waits for them, and re-layouts, body(): lax.scan(step_block, empty, (key_blocks, value_blocks, block_offsets))[0]  7.61 us
    all_to_all x1, starting transfers between devices, body(): lax.all_to_all(outgoing, 'batch', split_axis=0, concat_axis=0, tiled=True)  5.42 us
    all_to_all x1, starting transfers between devices, body(): lax.all_to_all(w_out, 'head', split_axis=1, concat_axis=0, tiled=True)  4.23 us
  transfers between devices with their start and end apart: 2, of which 1 were waited for; matrix products, arithmetic and copies ran while one was open for 8% of the time, Pallas kernels for 0%

commit v1 on v0

v1 whole, which is shorter than its diff:
```python
import functools
import math

import jax
import jax.numpy as jnp
from jax import lax
from jax.experimental import pallas as pl
from jax.experimental.pallas import tpu as pltpu
from jax.sharding import PartitionSpec as P

HD = 128
MESH = pl.DeviceIdType.MESH
QUERY, KEY, VALUE, UPDATE = 0, 1, 2, 3
FIRST_KINDS = (KEY, VALUE, QUERY)


def partner(me, mask, count):
    out = 0
    bit = 1
    while bit < count:
        out = out + lax.rem(lax.div(me, bit) + (mask // bit) % 2, 2) * bit
        bit *= 2
    return out


def kernel(sizes, shard_ref, slot_ref, hist_ref, ingest_ref, w_ref, out_ref,
           send_bufs, send_u, recv_bufs, recv_u, own_k, own_v, own_q, prev_k, prev_v,
           start_ref, att, gated, w_cols, mixed,
           z_send, z_recv, u_send, u_recv, c_send, c_recv, h_send, h_recv, w_send, w_recv):
    groups, ctxs, heads, per_owner, rows = sizes
    capacity = per_owner // 2
    window = ctxs // 2
    row_count = per_owner * rows
    my_group = lax.axis_index("batch")
    my_ctx = lax.axis_index("ctx")
    my_head = lax.axis_index("head")

    barrier = pltpu.get_barrier_semaphore()
    for axis, me, count in (("batch", my_group, groups), ("ctx", my_ctx, ctxs), ("head", my_head, heads)):
        for offset in range(1, count):
            pl.semaphore_signal(barrier, inc=1, device_id={axis: lax.rem(me + offset, count)}, device_id_type=MESH)

    slots = []
    for dst in range(groups):
        picked = [jnp.int32(0)] * capacity
        seen = jnp.int32(0)
        for j in range(per_owner):
            hit = shard_ref[dst, j] == my_group
            slot = slot_ref[dst, j]
            for k in range(capacity):
                picked[k] = jnp.where(hit & (seen == k), slot, picked[k])
            seen = seen + jnp.where(hit, 1, 0)
        slots.append(picked)

    sources = [shard_ref[my_group, j] for j in range(per_owner)]
    ranks, sides = [], []
    for j in range(per_owner):
        rank = jnp.int32(0)
        for i in range(j):
            rank = rank + jnp.where(sources[i] == sources[j], 1, 0)
        ranks.append(jnp.minimum(rank, capacity - 1))
        sides.append(jnp.where(sources[j] == sources[0], 0, 1))

    def split_kind(kind):
        width = 4 * rows
        row = lax.broadcasted_iota(jnp.int32, (rows, width), 0)
        col = lax.broadcasted_iota(jnp.int32, (rows, width), 1)
        pick = jnp.where(col == row * 4 + kind, 1.0, 0.0).astype(jnp.bfloat16)

        def one(dst, k):
            block = ingest_ref[slots[dst][k]]
            return jnp.dot(pick, block, preferred_element_type=jnp.float32).astype(jnp.bfloat16)

        return one

    masks = list(range(groups - 1, 0, -1))
    peers = {m: partner(my_group, m, groups) for m in masks}

    def fill(kind):
        one = split_kind(kind)
        for dst in range(groups):
            for k in range(capacity):
                if kind == UPDATE:
                    send_u[k, dst] = one(dst, k)
                else:
                    send_bufs[FIRST_KINDS.index(kind), dst, k] = one(dst, k)

    copies = {}

    def send(kind):
        if kind == UPDATE:
            for k in range(capacity):
                for m in masks:
                    copies[kind, k, m] = pltpu.make_async_remote_copy(
                        src_ref=send_u.at[k, peers[m]], dst_ref=recv_u[k].at[my_group],
                        send_sem=u_send.at[k, m], recv_sem=u_recv.at[k, m],
                        device_id={"batch": peers[m]}, device_id_type=MESH)
                    copies[kind, k, m].start()
                recv_u[k][my_group] = send_u[k, my_group]
            return
        n = FIRST_KINDS.index(kind)
        for m in masks:
            copies[kind, m] = pltpu.make_async_remote_copy(
                src_ref=send_bufs.at[n, peers[m]], dst_ref=recv_bufs[n].at[my_group],
                send_sem=z_send.at[n, m], recv_sem=z_recv.at[n, m],
                device_id={"batch": peers[m]}, device_id_type=MESH)
            copies[kind, m].start()
        recv_bufs[n][my_group] = send_bufs[n, my_group]

    def collect(kind, own_ref):
        n = FIRST_KINDS.index(kind)
        for m in masks:
            copies[kind, m].wait()
        for j in range(per_owner):
            own_ref[j * rows:(j + 1) * rows, :] = recv_bufs[n][sources[j], ranks[j]]

    fill(KEY)
    pl.semaphore_wait(barrier, groups + ctxs + heads - 3)
    send(KEY)
    fill(VALUE)
    send(VALUE)
    fill(QUERY)
    send(QUERY)
    fill(UPDATE)
    send(UPDATE)

    w_copies = []
    for offset in range(1, heads):
        to = lax.rem(my_head + offset, heads)
        copy = pltpu.make_async_remote_copy(
            src_ref=w_ref.at[:, pl.ds(pl.multiple_of(to * HD, HD), HD)], dst_ref=w_cols.at[my_head],
            send_sem=w_send.at[offset], recv_sem=w_recv.at[offset],
            device_id={"head": to}, device_id_type=MESH)
        copy.start()
        w_copies.append(copy)
    w_cols[my_head] = w_ref[:, pl.ds(pl.multiple_of(my_head * HD, HD), HD)]

    ends, total = [], jnp.int32(0)
    for u in range(hist_ref.shape[0]):
        total = total + hist_ref[u]
        ends.append(total)
    base = my_ctx * row_count
    position = base + lax.broadcasted_iota(jnp.int32, (row_count, HD), 0)
    first = jnp.zeros((row_count, HD), jnp.int32)
    for end in ends:
        first = jnp.where(position >= end, end, first)
    start_ref[...] = first - base

    def ctx_copy(n, own_ref, prev_ref, offset):
        return pltpu.make_async_remote_copy(
            src_ref=own_ref, dst_ref=prev_ref.at[offset - 1],
            send_sem=c_send.at[n, offset - 1], recv_sem=c_recv.at[n, offset - 1],
            device_id={"ctx": lax.rem(my_ctx + offset, ctxs)}, device_id_type=MESH)

    def push(n, own_ref, prev_ref):
        for offset in range(1, window + 1):
            @pl.when(my_ctx + offset < ctxs)
            def _():
                ctx_copy(n, own_ref, prev_ref, offset).start()

    collect(KEY, own_k)
    push(0, own_k, prev_k)
    collect(VALUE, own_v)
    push(1, own_v, prev_v)
    collect(QUERY, own_q)

    tile = 2 * rows if per_owner % 2 == 0 else rows
    tiles = row_count // tile
    half_scale = 0.5 / math.sqrt(HD)

    def attend(q, key_tile, value_tile, q_lo, k_lo, shift, causal):
        scores = lax.dot_general(q, key_tile, (((1,), (1,)), ((), ())), preferred_element_type=jnp.float32)
        half = scores * half_scale
        act = half + half * jnp.tanh(half)
        key_pos = lax.broadcasted_iota(jnp.int32, (tile, tile), 1) + (k_lo - shift)
        first_pos = jnp.concatenate([start_ref[q_lo:q_lo + tile, :]] * (tile // HD), axis=1)
        visible = key_pos >= first_pos
        if causal:
            visible = visible & (key_pos <= lax.broadcasted_iota(jnp.int32, (tile, tile), 0) + q_lo)
        weights = jnp.where(visible, act, 0.0).astype(jnp.bfloat16)
        return jnp.dot(weights, value_tile, preferred_element_type=jnp.float32)

    def put(i, value, add):
        for part in range(tile // rows):
            at = i * (tile // rows) + part
            piece = value[part * rows:(part + 1) * rows]
            att[at] = att[at] + piece if add else piece

    for i in range(tiles):
        q = own_q[i * tile:(i + 1) * tile, :]
        acc = None
        for t in range(i + 1):
            span = slice(t * tile, (t + 1) * tile)
            term = attend(q, own_k[span, :], own_v[span, :], i * tile, t * tile, 0, t == i)
            acc = term if acc is None else acc + term
        put(i, acc, False)
    for offset in range(1, window + 1):
        @pl.when(my_ctx >= offset)
        def _():
            ctx_copy(0, own_k, prev_k, offset).wait_recv()
            ctx_copy(1, own_v, prev_v, offset).wait_recv()
            for i in range(tiles):
                q = own_q[i * tile:(i + 1) * tile, :]
                acc = None
                for t in range(i if offset == window else 0, tiles):
                    span = slice(t * tile, (t + 1) * tile)
                    term = attend(q, prev_k[offset - 1, span, :], prev_v[offset - 1, span, :],
                                  i * tile, t * tile, offset * row_count, False)
                    acc = term if acc is None else acc + term
                put(i, acc, True)

    source_other = sources[0]
    for j in range(1, per_owner):
        source_other = jnp.where(sides[j] == 1, sources[j], source_other)
    side_source = (sources[0], source_other)
    h_copies = []
    for k in range(capacity):
        for m in masks:
            copies[UPDATE, k, m].wait()
        for side in range(2):
            at = jnp.int32(0)
            for j in range(per_owner):
                at = jnp.where((ranks[j] == k) & (sides[j] == side), j, at)
            rows_f32 = att[at]
            mean_square = jnp.mean(rows_f32 * rows_f32, axis=-1, keepdims=True)
            normed = rows_f32 * lax.rsqrt(mean_square + 1e-06)
            update = recv_u[k][side_source[side]].astype(jnp.float32)
            gated[k, my_head, side * rows:(side + 1) * rows, :] = (normed * update).astype(jnp.bfloat16)
        for offset in range(1, heads):
            copy = pltpu.make_async_remote_copy(
                src_ref=gated.at[k, my_head], dst_ref=gated.at[k, my_head],
                send_sem=h_send.at[k, offset], recv_sem=h_recv.at[k, offset],
                device_id={"head": lax.rem(my_head + offset, heads)}, device_id_type=MESH)
            copy.start()
            h_copies.append(copy)
    for copy in w_copies:
        copy.wait()
    for k in range(capacity):
        for copy in h_copies[k * (heads - 1):(k + 1) * (heads - 1)]:
            copy.wait()
        acc = None
        for h in range(heads):
            term = jnp.dot(gated[k, h], w_cols[h], preferred_element_type=jnp.float32)
            acc = term if acc is None else acc + term
        acc = acc.astype(jnp.bfloat16)
        for side in range(2):
            mixed[2 * k + side] = acc[side * rows:(side + 1) * rows]
    for j in range(per_owner):
        out_ref[j * rows:(j + 1) * rows, :] = mixed[2 * ranks[j] + sides[j]]
    for offset in range(1, window + 1):
        @pl.when(my_ctx + offset < ctxs)
        def _():
            ctx_copy(0, own_k, prev_k, offset).wait_send()
            ctx_copy(1, own_v, prev_v, offset).wait_send()


def body(ingest, src_shard, src_slot, hist_len, w_out):
    groups, ctxs, heads = (lax.axis_size(a) for a in ("batch", "ctx", "head"))
    slot_total, rows, kinds, width = ingest.shape[2:]
    per_owner = src_shard.shape[2]
    capacity = per_owner // 2
    window = ctxs // 2
    row_count = per_owner * rows
    bf16 = jnp.bfloat16
    dma = pltpu.SemaphoreType.DMA
    vmem = pl.BlockSpec(memory_space=pltpu.VMEM)
    smem = pl.BlockSpec(memory_space=pltpu.SMEM)
    mixed = pl.pallas_call(
        functools.partial(kernel, (groups, ctxs, heads, per_owner, rows)),
        out_shape=jax.ShapeDtypeStruct((row_count, width), bf16),
        in_specs=[smem, smem, smem, vmem, vmem],
        out_specs=vmem,
        scratch_shapes=[
            pltpu.VMEM((3, groups, capacity, rows, width), bf16),
            pltpu.VMEM((capacity, groups, rows, width), bf16),
            [pltpu.VMEM((groups, capacity, rows, width), bf16)] * 3,
            [pltpu.VMEM((groups, rows, width), bf16)] * capacity,
            pltpu.VMEM((row_count, width), bf16),
            pltpu.VMEM((row_count, width), bf16),
            pltpu.VMEM((row_count, width), bf16),
            pltpu.VMEM((window, row_count, width), bf16),
            pltpu.VMEM((window, row_count, width), bf16),
            pltpu.VMEM((row_count, width), jnp.int32),
            pltpu.VMEM((per_owner, rows, width), jnp.float32),
            pltpu.VMEM((capacity, heads, 2 * rows, width), bf16),
            pltpu.VMEM((heads, width, width), bf16),
            pltpu.VMEM((per_owner, rows, width), bf16),
            dma((3, groups)), dma((3, groups)),
            dma((capacity, groups)), dma((capacity, groups)),
            dma((2, window)), dma((2, window)),
            dma((capacity, heads)), dma((capacity, heads)),
            dma((heads,)), dma((heads,)),
        ],
        compiler_params=pltpu.CompilerParams(
            collective_id=0, has_side_effects=True, vmem_limit_bytes=56 * 1024 * 1024),
    )(src_shard[0], src_slot[0], hist_len[0],
      ingest.reshape(slot_total, rows * kinds, width), w_out)
    return mixed[None]


def solution(mesh):
    in_specs = (
        P("ctx", "batch", None, None, None, "head"),
        P("ctx", None, None),
        P("ctx", None, None),
        P("batch", None),
        P("head", None),
    )
    out_specs = P("batch", "ctx", "head")
    return jax.shard_map(body, mesh=mesh, in_specs=in_specs, out_specs=out_specs, check_vma=False)
```

time: 110 us -> 49.4 us (0.45)
  Pallas kernels: 0 us -> 47.6 us
  waiting for transfers between devices: 33.6 us -> 0 us
  blocking collectives: 25.6 us -> 0 us
  local copies, waits for them, and re-layouts: 17.5 us -> 1.62 us
  matrix products: 12.7 us -> 0 us
  other arithmetic: 9.72 us -> 0 us
  starting transfers between devices: 9.66 us -> 0 us
    pallas_call x0 -> x1, Pallas kernels: none -> 47.6 us  [body(): pl.pallas_call(functools.partial(kernel, (groups, ctxs, heads, per_owner,...]
    all_to_all x2 -> x0, waiting for transfers between devices: 33.6 us -> none  [the longest x1 33.6 us: body(): lax.all_to_all(outgoing, 'batch', split_axis=0, concat_axis=0, tiled=True)]
    all_gather x3 -> x0, blocking collectives: 25.6 us -> none  [the longest x1 9.14 us: body(): key_rows = lax.all_gather(key_part, 'ctx', axis=0, tiled=True)]
    dot_general x7 -> x0, matrix products: 12.7 us -> none  [the longest x6 11.8 us: tile_update(): jnp.einsum('hqk,khd->qhd', weights, value_heads, preferred_element_type=j...]
    all_to_all x2 -> x0, starting transfers between devices: 9.66 us -> none  [the longest x1 5.42 us: body(): lax.all_to_all(outgoing, 'batch', split_axis=0, concat_axis=0, tiled=True)]
    dynamic_slice x6 -> x0, local copies, waits for them, and re-layouts: 7.61 us -> none  [body(): lax.scan(step_block, empty, (key_blocks, value_blocks, block_offsets))[0]]
    gather x3 -> x0, local copies, waits for them, and re-layouts: 4.64 us -> none  [the longest x2 2.73 us: body(): jnp.take(incoming.reshape(groups * capacity, block_rows, kinds, local_wid...]
    add x13 -> x0, other arithmetic: 3.82 us -> none  [the longest x6 3.79 us: tile_update(): key_pos = offset + jnp.arange(key_count, dtype=jnp.int32)]
  transfers between devices with their start and end apart: 2 -> 0, of which waited for: 1 -> 0; matrix products, arithmetic and copies ran while one was open for 8% -> 0% of each run, Pallas kernels for 0% -> 0%
where the time goes in v1:
time: 49.4 us; the launch traced here: 49.3 us
  Pallas kernels  47.6 us (96%)
  local copies, waits for them, and re-layouts  1.62 us (3%)
    pallas_call x1, Pallas kernels, body(): pl.pallas_call(functools.partial(kernel, (groups, ctxs, heads, per_owner,...  47.6 us
    unnamed x1, local copies, waits for them, and re-layouts  1.62 us

profile of v1, /device:TPU:0, one launch (start us, length us, event | category | flops | bytes accessed | tf_op | source)
XLA Modules:
  0.0 49.3 jit_solution(2857399233352051012)
XLA Ops:
  0.0 47.6 %shard_map.55 = bf16[768,128]{1,0:T(8,128)(2,1)} custom-call(s32[4,6]{1,0:T(4,128)} %bitcast.7, s32[4,6]{1,0:T(4,128)} %bitcast.8, s32[4]{0:T(128)} %bitcast.9, bf16[12,512,128]{2,1,0:T(8,128)(2,1)} %bitcast.5, bf16[128,256]{1,0:T(8,128)(2,1)} %w_ref.1), custom_call_target="tpu_custom_call" | custom-call | tf_op jit(solution)/shard_map/pallas_call | solution.py:268
  47.6 1.6 %copy.7 = bf16[1,768,128]{2,1,0:T(8,128)(2,1)} copy(bf16[1,768,128]{2,1,0:T(8,128)(2,1)} %bitcast.6) | data formatting | bytes 393216

commit v2 on v1

--- a/solution.py
+++ b/solution.py
@@ -23,12 +23,20 @@
     return out
 
 
-def kernel(sizes, shard_ref, slot_ref, hist_ref, ingest_ref, w_ref, out_ref,
+def update_chunks(capacity, rows):
+    half = rows // 2
+    return [(k, 0, rows) for k in range(capacity - 1)] + [(capacity - 1, 0, half), (capacity - 1, half, half)]
+
+
+def kernel(sizes, shard_ref, slot_ref, hist_ref, ingest_hbm, w_ref, out_ref,
+           ingest_ref,
            send_bufs, send_u, recv_bufs, recv_u, own_k, own_v, own_q, prev_k, prev_v,
            start_ref, att, gated, w_cols, mixed,
-           z_send, z_recv, u_send, u_recv, c_send, c_recv, h_send, h_recv, w_send, w_recv):
+           z_send, z_recv, u_send, u_recv, c_send, c_recv, h_send, h_recv, w_send, w_recv,
+           ingest_sem, from_low, from_high):
     groups, ctxs, heads, per_owner, rows = sizes
     capacity = per_owner // 2
+    chunks = update_chunks(capacity, rows)
     window = ctxs // 2
     row_count = per_owner * rows
     my_group = lax.axis_index("batch")
@@ -36,9 +44,21 @@
     my_head = lax.axis_index("head")
 
     barrier = pltpu.get_barrier_semaphore()
-    for axis, me, count in (("batch", my_group, groups), ("ctx", my_ctx, ctxs), ("head", my_head, heads)):
+    ingest_copy = pltpu.make_async_copy(ingest_hbm, ingest_ref, ingest_sem)
+    ingest_copy.start()
+    for axis, me, count in (("ctx", my_ctx, ctxs), ("head", my_head, heads)):
         for offset in range(1, count):
             pl.semaphore_signal(barrier, inc=1, device_id={axis: lax.rem(me + offset, count)}, device_id_type=MESH)
+    has_low, has_high = my_group > 0, my_group < groups - 1
+
+    def tell(there, semaphore, to):
+        @pl.when(there)
+        def _():
+            pl.semaphore_signal(semaphore, inc=1, device_id={"batch": to}, device_id_type=MESH)
+
+    tell(has_low, barrier, my_group - 1)
+    tell(has_high, barrier, my_group + 1)
+    neighbours = jnp.where(has_low, 1, 0) + jnp.where(has_high, 1, 0)
 
     slots = []
     for dst in range(groups):
@@ -81,7 +101,10 @@
         for dst in range(groups):
             for k in range(capacity):
                 if kind == UPDATE:
-                    send_u[k, dst] = one(dst, k)
+                    block = one(dst, k)
+                    for c, (of, low, size) in enumerate(chunks):
+                        if of == k:
+                            send_u[c][dst] = block[low:low + size]
                 else:
                     send_bufs[FIRST_KINDS.index(kind), dst, k] = one(dst, k)
 
@@ -89,14 +112,14 @@
 
     def send(kind):
         if kind == UPDATE:
-            for k in range(capacity):
+            for c in range(len(chunks)):
                 for m in masks:
-                    copies[kind, k, m] = pltpu.make_async_remote_copy(
-                        src_ref=send_u.at[k, peers[m]], dst_ref=recv_u[k].at[my_group],
-                        send_sem=u_send.at[k, m], recv_sem=u_recv.at[k, m],
+                    copies[kind, c, m] = pltpu.make_async_remote_copy(
+                        src_ref=send_u[c].at[peers[m]], dst_ref=recv_u[c].at[my_group],
+                        send_sem=u_send.at[c, m], recv_sem=u_recv.at[c, m],
                         device_id={"batch": peers[m]}, device_id_type=MESH)
-                    copies[kind, k, m].start()
-                recv_u[k][my_group] = send_u[k, my_group]
+                    copies[kind, c, m].start()
+                recv_u[c][my_group] = send_u[c][my_group]
             return
         n = FIRST_KINDS.index(kind)
         for m in masks:
@@ -104,7 +127,8 @@
                 src_ref=send_bufs.at[n, peers[m]], dst_ref=recv_bufs[n].at[my_group],
                 send_sem=z_send.at[n, m], recv_sem=z_recv.at[n, m],
                 device_id={"batch": peers[m]}, device_id_type=MESH)
-            copies[kind, m].start()
+            if kind != KEY:
+                copies[kind, m].start()
         recv_bufs[n][my_group] = send_bufs[n, my_group]
 
     def collect(kind, own_ref):
@@ -114,10 +138,35 @@
         for j in range(per_owner):
             own_ref[j * rows:(j + 1) * rows, :] = recv_bufs[n][sources[j], ranks[j]]
 
+    def start_at(distance):
+        for m in masks:
+            @pl.when((peers[m] - my_group == distance) | (my_group - peers[m] == distance))
+            def _():
+                copies[KEY, m].start()
+
+    def hear(distance):
+        for there, semaphore in ((my_group >= distance, from_low), (my_group + distance < groups, from_high)):
+            @pl.when(there)
+            def _():
+                pl.semaphore_wait(semaphore.at[distance], 1)
+
+    def pass_on(distance):
+        tell((my_group >= distance) & has_high, from_low.at[distance + 1], my_group + 1)
+        tell((my_group + distance < groups) & has_low, from_high.at[distance + 1], my_group - 1)
+
+    ingest_copy.wait()
     fill(KEY)
-    pl.semaphore_wait(barrier, groups + ctxs + heads - 3)
+    pl.semaphore_wait(barrier, neighbours + ctxs + heads - 2)
+    if groups > 2:
+        pass_on(1)
     send(KEY)
+    start_at(1)
     fill(VALUE)
+    for distance in range(2, groups):
+        hear(distance)
+        if distance + 1 < groups:
+            pass_on(distance)
+        start_at(distance)
     send(VALUE)
     fill(QUERY)
     send(QUERY)
@@ -214,37 +263,37 @@
         source_other = jnp.where(sides[j] == 1, sources[j], source_other)
     side_source = (sources[0], source_other)
     h_copies = []
-    for k in range(capacity):
+    for c, (k, low, size) in enumerate(chunks):
         for m in masks:
-            copies[UPDATE, k, m].wait()
+            copies[UPDATE, c, m].wait()
         for side in range(2):
             at = jnp.int32(0)
             for j in range(per_owner):
                 at = jnp.where((ranks[j] == k) & (sides[j] == side), j, at)
-            rows_f32 = att[at]
+            rows_f32 = att[at, low:low + size, :]
             mean_square = jnp.mean(rows_f32 * rows_f32, axis=-1, keepdims=True)
             normed = rows_f32 * lax.rsqrt(mean_square + 1e-06)
-            update = recv_u[k][side_source[side]].astype(jnp.float32)
-            gated[k, my_head, side * rows:(side + 1) * rows, :] = (normed * update).astype(jnp.bfloat16)
+            update = recv_u[c][side_source[side]].astype(jnp.float32)
+            gated[c][my_head, side * size:(side + 1) * size, :] = (normed * update).astype(jnp.bfloat16)
         for offset in range(1, heads):
             copy = pltpu.make_async_remote_copy(
-                src_ref=gated.at[k, my_head], dst_ref=gated.at[k, my_head],
-                send_sem=h_send.at[k, offset], recv_sem=h_recv.at[k, offset],
+                src_ref=gated[c].at[my_head], dst_ref=gated[c].at[my_head],
+                send_sem=h_send.at[c, offset], recv_sem=h_recv.at[c, offset],
                 device_id={"head": lax.rem(my_head + offset, heads)}, device_id_type=MESH)
             copy.start()
             h_copies.append(copy)
     for copy in w_copies:
         copy.wait()
-    for k in range(capacity):
-        for copy in h_copies[k * (heads - 1):(k + 1) * (heads - 1)]:
+    for c, (k, low, size) in enumerate(chunks):
+        for copy in h_copies[c * (heads - 1):(c + 1) * (heads - 1)]:
             copy.wait()
         acc = None
         for h in range(heads):
-            term = jnp.dot(gated[k, h], w_cols[h], preferred_element_type=jnp.float32)
+            term = jnp.dot(gated[c][h], w_cols[h], preferred_element_type=jnp.float32)
             acc = term if acc is None else acc + term
         acc = acc.astype(jnp.bfloat16)
         for side in range(2):
-            mixed[2 * k + side] = acc[side * rows:(side + 1) * rows]
+            mixed[2 * k + side, low:low + size, :] = acc[side * size:(side + 1) * size]
     for j in range(per_owner):
         out_ref[j * rows:(j + 1) * rows, :] = mixed[2 * ranks[j] + sides[j]]
     for offset in range(1, window + 1):
@@ -259,6 +308,7 @@
     slot_total, rows, kinds, width = ingest.shape[2:]
     per_owner = src_shard.shape[2]
     capacity = per_owner // 2
+    chunks = update_chunks(capacity, rows)
     window = ctxs // 2
     row_count = per_owner * rows
     bf16 = jnp.bfloat16
@@ -268,13 +318,14 @@
     mixed = pl.pallas_call(
         functools.partial(kernel, (groups, ctxs, heads, per_owner, rows)),
         out_shape=jax.ShapeDtypeStruct((row_count, width), bf16),
-        in_specs=[smem, smem, smem, vmem, vmem],
+        in_specs=[smem, smem, smem, pl.BlockSpec(memory_space=pl.ANY), vmem],
         out_specs=vmem,
         scratch_shapes=[
+            pltpu.VMEM((slot_total, rows * kinds, width), bf16),
             pltpu.VMEM((3, groups, capacity, rows, width), bf16),
-            pltpu.VMEM((capacity, groups, rows, width), bf16),
+            [pltpu.VMEM((groups, size, width), bf16) for _, _, size in chunks],
             [pltpu.VMEM((groups, capacity, rows, width), bf16)] * 3,
-            [pltpu.VMEM((groups, rows, width), bf16)] * capacity,
+            [pltpu.VMEM((groups, size, width), bf16) for _, _, size in chunks],
             pltpu.VMEM((row_count, width), bf16),
             pltpu.VMEM((row_count, width), bf16),
             pltpu.VMEM((row_count, width), bf16),
@@ -282,14 +333,15 @@
             pltpu.VMEM((window, row_count, width), bf16),
             pltpu.VMEM((row_count, width), jnp.int32),
             pltpu.VMEM((per_owner, rows, width), jnp.float32),
-            pltpu.VMEM((capacity, heads, 2 * rows, width), bf16),
+            [pltpu.VMEM((heads, 2 * size, width), bf16) for _, _, size in chunks],
             pltpu.VMEM((heads, width, width), bf16),
             pltpu.VMEM((per_owner, rows, width), bf16),
             dma((3, groups)), dma((3, groups)),
-            dma((capacity, groups)), dma((capacity, groups)),
+            dma((len(chunks), groups)), dma((len(chunks), groups)),
             dma((2, window)), dma((2, window)),
-            dma((capacity, heads)), dma((capacity, heads)),
+            dma((len(chunks), heads)), dma((len(chunks), heads)),
             dma((heads,)), dma((heads,)),
+            dma, pltpu.SemaphoreType.REGULAR((groups,)), pltpu.SemaphoreType.REGULAR((groups,)),
         ],
         compiler_params=pltpu.CompilerParams(
             collective_id=0, has_side_effects=True, vmem_limit_bytes=56 * 1024 * 1024),

time: 49.4 us -> 48.9 us (0.990)
  Pallas kernels: 47.6 us -> 47.1 us
    pallas_call x1, Pallas kernels: 47.6 us -> 47.1 us  [body(): pl.pallas_call(functools.partial(kernel, (groups, ctxs, heads, per_owner,...]
where the time goes in v2:
time: 48.9 us; the launch traced here: 48.7 us
  Pallas kernels  47.1 us (96%)
  local copies, waits for them, and re-layouts  1.62 us (3%)
    pallas_call x1, Pallas kernels, body(): pl.pallas_call(functools.partial(kernel, (groups, ctxs, heads, per_owner,...  47.1 us
    unnamed x1, local copies, waits for them, and re-layouts  1.62 us

profile of v2, /device:TPU:0, one launch (start us, length us, event | category | flops | bytes accessed | tf_op | source)
XLA Modules:
  0.0 48.7 jit_solution(5172602072446825483)
XLA Ops:
  0.0 47.1 %shard_map.55 = bf16[768,128]{1,0:T(8,128)(2,1)} custom-call(s32[4,6]{1,0:T(4,128)} %bitcast.7, s32[4,6]{1,0:T(4,128)} %bitcast.8, s32[4]{0:T(128)} %bitcast.9, bf16[12,512,128]{2,1,0:T(8,128)(2,1)} %bitcast.5, bf16[128,256]{1,0:T(8,128)(2,1)} %w_ref.1), custom_call_target="tpu_custom_call" | custom-call | tf_op jit(solution)/shard_map/pallas_call | solution.py:318
  47.1 1.6 %copy.7 = bf16[1,768,128]{2,1,0:T(8,128)(2,1)} copy(bf16[1,768,128]{2,1,0:T(8,128)(2,1)} %bitcast.6) | data formatting | bytes 393216

commit v3 on v2

--- a/solution.py
+++ b/solution.py
@@ -28,7 +28,8 @@
     return [(k, 0, rows) for k in range(capacity - 1)] + [(capacity - 1, 0, half), (capacity - 1, half, half)]
 
 
-def kernel(sizes, shard_ref, slot_ref, hist_ref, ingest_hbm, w_ref, out_ref,
+def kernel(sizes, shard_hbm, slot_hbm, hist_hbm, ingest_hbm, w_hbm, out_ref,
+           shard_ref, slot_ref, hist_ref, w_ref, local_sems,
            ingest_ref,
            send_bufs, send_u, recv_bufs, recv_u, own_k, own_v, own_q, prev_k, prev_v,
            start_ref, att, gated, w_cols, mixed,
@@ -46,6 +47,10 @@
     barrier = pltpu.get_barrier_semaphore()
     ingest_copy = pltpu.make_async_copy(ingest_hbm, ingest_ref, ingest_sem)
     ingest_copy.start()
+    local_copies = [pltpu.make_async_copy(src, dst, local_sems.at[i]) for i, (src, dst) in enumerate((
+        (shard_hbm, shard_ref), (slot_hbm, slot_ref), (hist_hbm, hist_ref), (w_hbm, w_ref)))]
+    for copy in local_copies:
+        copy.start()
     for axis, me, count in (("ctx", my_ctx, ctxs), ("head", my_head, heads)):
         for offset in range(1, count):
             pl.semaphore_signal(barrier, inc=1, device_id={axis: lax.rem(me + offset, count)}, device_id_type=MESH)
@@ -60,6 +65,8 @@
     tell(has_high, barrier, my_group + 1)
     neighbours = jnp.where(has_low, 1, 0) + jnp.where(has_high, 1, 0)
 
+    for copy in local_copies:
+        copy.wait()
     slots = []
     for dst in range(groups):
         picked = [jnp.int32(0)] * capacity
@@ -314,13 +321,14 @@
     bf16 = jnp.bfloat16
     dma = pltpu.SemaphoreType.DMA
     vmem = pl.BlockSpec(memory_space=pltpu.VMEM)
-    smem = pl.BlockSpec(memory_space=pltpu.SMEM)
     mixed = pl.pallas_call(
         functools.partial(kernel, (groups, ctxs, heads, per_owner, rows)),
         out_shape=jax.ShapeDtypeStruct((row_count, width), bf16),
-        in_specs=[smem, smem, smem, pl.BlockSpec(memory_space=pl.ANY), vmem],
+        in_specs=[pl.BlockSpec(memory_space=pl.ANY)] * 5,
         out_specs=vmem,
         scratch_shapes=[
+            pltpu.SMEM(src_shard.shape[1:], jnp.int32), pltpu.SMEM(src_slot.shape[1:], jnp.int32),
+            pltpu.SMEM(hist_len.shape[1:], jnp.int32), pltpu.VMEM(w_out.shape, bf16), dma((4,)),
             pltpu.VMEM((slot_total, rows * kinds, width), bf16),
             pltpu.VMEM((3, groups, capacity, rows, width), bf16),
             [pltpu.VMEM((groups, size, width), bf16) for _, _, size in chunks],

time: 48.9 us -> 48.1 us (0.984)
  Pallas kernels: 47.1 us -> 46.3 us
    pallas_call x1, Pallas kernels: 47.1 us -> 46.3 us  [body(): pl.pallas_call(functools.partial(kernel, (groups, ctxs, heads, per_owner,...]
where the time goes in v3:
time: 48.1 us; the launch traced here: 47.9 us
  Pallas kernels  46.3 us (96%)
  local copies, waits for them, and re-layouts  1.62 us (3%)
    pallas_call x1, Pallas kernels, body(): pl.pallas_call(functools.partial(kernel, (groups, ctxs, heads, per_owner,...  46.3 us
    unnamed x1, local copies, waits for them, and re-layouts  1.62 us

profile of v3, /device:TPU:0, one launch (start us, length us, event | category | flops | bytes accessed | tf_op | source)
XLA Modules:
  0.0 47.9 jit_solution(7602410434062717400)
XLA Ops:
  0.0 46.3 %shard_map.55 = bf16[768,128]{1,0:T(8,128)(2,1)} custom-call(s32[4,6]{1,0:T(4,128)} %bitcast.7, s32[4,6]{1,0:T(4,128)} %bitcast.8, s32[4]{0:T(128)} %bitcast.9, bf16[12,512,128]{2,1,0:T(8,128)(2,1)} %bitcast.5, bf16[128,256]{1,0:T(8,128)(2,1)} %w_hbm.1), custom_call_target="tpu_custom_call" | custom-call | tf_op jit(solution)/shard_map/pallas_call | solution.py:324
  46.3 1.6 %copy.7 = bf16[1,768,128]{2,1,0:T(8,128)(2,1)} copy(bf16[1,768,128]{2,1,0:T(8,128)(2,1)} %bitcast.6) | data formatting | bytes 393216

commit v4 on v3

--- a/solution.py
+++ b/solution.py
@@ -323,7 +323,7 @@
     vmem = pl.BlockSpec(memory_space=pltpu.VMEM)
     mixed = pl.pallas_call(
         functools.partial(kernel, (groups, ctxs, heads, per_owner, rows)),
-        out_shape=jax.ShapeDtypeStruct((row_count, width), bf16),
+        out_shape=pltpu.VMEM((row_count, width), bf16),
         in_specs=[pl.BlockSpec(memory_space=pl.ANY)] * 5,
         out_specs=vmem,
         scratch_shapes=[

time: 48.1 us -> 46.5 us (0.967)
  local copies, waits for them, and re-layouts: 1.62 us -> 0.68 us
  Pallas kernels: 46.3 us -> 45.6 us
    unnamed x1, local copies, waits for them, and re-layouts: 1.62 us -> 0.68 us
    pallas_call x1, Pallas kernels: 46.3 us -> 45.6 us  [body(): pl.pallas_call(functools.partial(kernel, (groups, ctxs, heads, per_owner,...]
where the time goes in v4:
time: 46.5 us; the launch traced here: 46.3 us
  Pallas kernels  45.6 us (98%)
  local copies, waits for them, and re-layouts  0.68 us (1%)
    pallas_call x1, Pallas kernels, body(): pl.pallas_call(functools.partial(kernel, (groups, ctxs, heads, per_owner,...  45.6 us

profile of v4, /device:TPU:0, one launch (start us, length us, event | category | flops | bytes accessed | tf_op | source)
XLA Modules:
  0.0 46.3 jit_solution(7310177687811835325)
XLA Ops:
  0.0 45.6 %shard_map.55 = bf16[768,128]{1,0:T(8,128)(2,1)S(1)} custom-call(s32[4,6]{1,0:T(4,128)} %bitcast.7, s32[4,6]{1,0:T(4,128)} %bitcast.8, s32[4]{0:T(128)} %bitcast.9, bf16[12,512,128]{2,1,0:T(8,128)(2,1)} %bitcast.6, bf16[128,256]{1,0:T(8,128)(2,1)} %w_hbm.1), custom_call_target="tpu_custom_call" | custom-call | tf_op jit(solution)/shard_map/pallas_call | solution.py:324
  45.6 0.7 %copy.7 = bf16[1,768,128]{2,1,0:T(8,128)(2,1)} copy(bf16[1,768,128]{2,1,0:T(8,128)(2,1)S(1)} %bitcast.5) | data formatting | bytes 393216

commit v5 on v4

--- a/solution.py
+++ b/solution.py
@@ -269,6 +269,10 @@
     for j in range(1, per_owner):
         source_other = jnp.where(sides[j] == 1, sources[j], source_other)
     side_source = (sources[0], source_other)
+    for j in range(per_owner):
+        rows_f32 = att[j]
+        mean_square = jnp.mean(rows_f32 * rows_f32, axis=-1, keepdims=True)
+        att[j] = rows_f32 * lax.rsqrt(mean_square + 1e-06)
     h_copies = []
     for c, (k, low, size) in enumerate(chunks):
         for m in masks:
@@ -277,9 +281,7 @@
             at = jnp.int32(0)
             for j in range(per_owner):
                 at = jnp.where((ranks[j] == k) & (sides[j] == side), j, at)
-            rows_f32 = att[at, low:low + size, :]
-            mean_square = jnp.mean(rows_f32 * rows_f32, axis=-1, keepdims=True)
-            normed = rows_f32 * lax.rsqrt(mean_square + 1e-06)
+            normed = att[at, low:low + size, :]
             update = recv_u[c][side_source[side]].astype(jnp.float32)
             gated[c][my_head, side * size:(side + 1) * size, :] = (normed * update).astype(jnp.bfloat16)
         for offset in range(1, heads):

time: 46.5 us -> 46.5 us (level)
  no operation moved by 1% of the time
where the time goes in v5:
time: 46.5 us; the launch traced here: 46.4 us
  Pallas kernels  45.7 us (98%)
  local copies, waits for them, and re-layouts  0.68 us (1%)
    pallas_call x1, Pallas kernels, body(): pl.pallas_call(functools.partial(kernel, (groups, ctxs, heads, per_owner,...  45.7 us

profile of v5, /device:TPU:0, one launch (start us, length us, event | category | flops | bytes accessed | tf_op | source)
XLA Modules:
  0.0 46.4 jit_solution(5000151397858053992)
XLA Ops:
  0.0 45.7 %shard_map.55 = bf16[768,128]{1,0:T(8,128)(2,1)S(1)} custom-call(s32[4,6]{1,0:T(4,128)} %bitcast.7, s32[4,6]{1,0:T(4,128)} %bitcast.8, s32[4]{0:T(128)} %bitcast.9, bf16[12,512,128]{2,1,0:T(8,128)(2,1)} %bitcast.6, bf16[128,256]{1,0:T(8,128)(2,1)} %w_hbm.1), custom_call_target="tpu_custom_call" | custom-call | tf_op jit(solution)/shard_map/pallas_call | solution.py:326
  45.7 0.7 %copy.7 = bf16[1,768,128]{2,1,0:T(8,128)(2,1)} copy(bf16[1,768,128]{2,1,0:T(8,128)(2,1)S(1)} %bitcast.5) | data formatting | bytes 393216
